TPU v7x, 128 devices: a whole 4x4x4 slice. The times are simulated.
128 devices in a mesh: cls: 8 (over y, core), mem: 16 (over z, x).
Axes of the slice: x: 4, y: 4, z: 4, core: 2. Of those that a mesh axis runs over, the one named last changes fastest.
Arguments:
- images: bfloat16 [3072, 65536], P(('cls', 'mem')), may hold values from -6 to 6
- owner_group: int32 [3072, 1], P(('cls', 'mem')), may hold values from 0 to 7; in each aligned block of 24 rows (0 to 23, 24 to 47, ...) at most 6 rows name the same one
- bin_in_group: int32 [3072], P(('cls', 'mem')), may hold values from 0 to 7
- defocus: bfloat16 [3072], P(('cls', 'mem')), may hold values from 0.5 to 2
- projections: bfloat16 [64, 65536], P('cls'), may hold values from -6 to 6
- sketch_weight: bfloat16 [64, 48], replicated, may hold values from -0.875 to 0.875
Outputs:
- basis: bfloat16 [8, 64, 65536], P('cls', None, 'mem')
Inputs may be any that keep to these rules, and one draw needn't show every extreme that they name: `owner_group`: in the particles of one device no class group is named more than 6 times, and 6 is reached on some device.
All inputs are finite; a program needn't handle non-finite values.
Results may differ from a plain program's by a relative error of at most 0.012.
The roundings to bfloat16 on the way count: a program that leaves them out, or rounds other values in their place, can miss the bound.
Values may be sent and summed in bfloat16 or wider, within the bound.
A program may use at most 128 MiB of HBM per device.

v0:
```python
import functools
import math

import jax
import jax.numpy as jnp
import numpy as np
from jax import lax
from jax.experimental import pallas as pl
from jax.experimental.pallas import tpu as pltpu
from jax.sharding import PartitionSpec as P

SIDE = 256
CAP = 6
N_CLS = 8
N_MEM = 16
RANK = 64
P_DEV = 24
P_PAD = 32
PIX = 65536
WIDTH = PIX // N_MEM
CHUNKS = 8
W = WIDTH // CHUNKS
PART = N_MEM * CAP
SLOTS = N_CLS * PART
ROWS = N_MEM * RANK
COLS = N_MEM * P_PAD
BLOCK = 256
PAIRS = [(i, j) for i in range(SLOTS // BLOCK) for j in range(i, SLOTS // BLOCK)]
QUADS = ROWS // BLOCK
QUAD_PAIRS = [(i, j) for i in range(QUADS) for j in range(i, QUADS)]
HALF = len(PAIRS) * BLOCK // 2
FOURTH = HALF // 4
LAST = FOURTH // 4
MESH = pl.DeviceIdType.MESH


def sine_terms():
    nodes = np.cos(np.pi * (np.arange(400) + 0.5) / 400) * 0.5
    basis = np.stack([nodes ** (2 * i + 1) for i in range(6)], axis=1)
    wanted = -math.sqrt(1.01) * np.sin(2 * np.pi * nodes)
    return [float(v) for v in np.linalg.lstsq(basis, wanted, rcond=None)[0]]


SINE = sine_terms()
ROUND = 12582912.0
STRIP = 16


def narrow(value):
    return value.astype(jnp.bfloat16)


def dot(a, b):
    return jnp.dot(narrow(a), narrow(b), preferred_element_type=jnp.float32)


def dot_t(a, b):
    return lax.dot_general(narrow(a), narrow(b), (((1,), (1,)), ((), ())), preferred_element_type=jnp.float32)


def normalise(gram):
    n = gram.shape[0]
    row = lax.broadcasted_iota(jnp.int32, (n, n), 0)
    col = lax.broadcasted_iota(jnp.int32, (n, n), 1)
    diag = jnp.sum(jnp.where(row == col, gram, 0.0), axis=0, keepdims=True)
    same = lax.shift_right_logical(row, 6) == lax.shift_right_logical(col, 6)
    total = jnp.sum(jnp.where(same, diag, 0.0), axis=1, keepdims=True) + 1e-06
    g = jnp.where(same, gram, 0.0) / total
    g2 = dot(g, g)
    rest = -2.4375 * g + 1.6875 * g2 + dot(g2, -0.5625 * g + 0.0625 * g2)
    return rest, jnp.sqrt(float(PIX) / total)


def advance(gram, factor):
    rest, scale = normalise(gram)
    return scale * (2.25 * factor + dot(rest, factor))


def merged_factors(block):
    row = lax.broadcasted_iota(jnp.int32, (BLOCK, BLOCK), 0)
    col = lax.broadcasted_iota(jnp.int32, (BLOCK, BLOCK), 1)
    ident = jnp.where(row == col, 1.0, 0.0)
    chain = []
    for q in range(QUADS):
        rest, scale = normalise(block(q, q).astype(jnp.float32))
        chain.append(scale * (2.25 * ident + rest))
    for level in range(2):
        step = RANK << level
        for q in range(QUADS):
            d = chain[q]
            swapped = jnp.concatenate([d[a ^ step:(a ^ step) + step] for a in range(0, BLOCK, step)], axis=0)
            joined = d + swapped
            chain[q] = advance(dot_t(dot(joined, block(q, q)), joined), joined)
    chain = [d[:RANK] for d in chain]
    size = 2
    while size <= QUADS:
        for first in range(0, QUADS, size):
            group = range(first, first + size)
            gram = None
            for j in group:
                t = None
                for i in group:
                    part = dot(chain[i], block(i, j)) if i <= j else dot_t(chain[i], block(j, i))
                    t = part if t is None else t + part
                part = dot_t(t, chain[j])
                gram = part if gram is None else gram + part
            rest, scale = normalise(gram)
            for i in group:
                chain[i] = scale * (2.25 * chain[i] + dot(rest, chain[i]))
        size *= 2
    return chain


def kernel(images, owner, bins, defocus, proj, weight, spread, out, x_buf, m_own, m_buf, sel, send, recv, smeta, rmeta,
           pj, wt, focus, table, grid_q, chosen, res, acc, packed, first_in, mid, second_in, gath, turned, gram, coef,
           xs, xr, ms, mr, ys, yr, pm, s1, r1, s2, r2, s3, r3, s4, r4):
    cls = lax.axis_index("cls")
    mem = lax.axis_index("mem")
    y, core = cls // 2, cls % 2
    up, down, far = (y + 1) % 4, (y + 3) % 4, (y + 2) % 4
    z, x = mem // 4, mem % 4

    barrier = pltpu.get_barrier_semaphore()

    def peer(o):
        return ((z + o // 4) % 4) * 4 + (x + o % 4) % 4

    x_buf[...] = jnp.zeros_like(x_buf)
    m_buf[...] = jnp.zeros_like(m_buf)

    @pl.loop(1, N_MEM)
    def _(o):
        pl.semaphore_signal(barrier, inc=1, device_id={"mem": peer(o)}, device_id_type=MESH)

    others = [far * 2, far * 2 + 1, up * 2, down * 2 + 1, up * 2 + 1, down * 2, y * 2 + 1 - core]
    for other in others:
        pl.semaphore_signal(barrier, inc=1, device_id={"cls": other}, device_id_type=MESH)


    lane = lax.broadcasted_iota(jnp.int32, (P_DEV, 128), 1)
    row = lax.broadcasted_iota(jnp.int32, (P_DEV, P_DEV), 0)
    col = lax.broadcasted_iota(jnp.int32, (P_DEV, P_DEV), 1)
    def upright(values):
        return jnp.sum(jnp.where(row == col, values.astype(jnp.float32), 0.0), axis=1, keepdims=True)

    who = upright(owner[...])
    onehot = jnp.where(lane.astype(jnp.float32) == who, 1.0, 0.0)
    before = dot(jnp.where(col < row, 1.0, 0.0), onehot)
    rank = jnp.sum(onehot * before, axis=1, keepdims=True)
    meta = jnp.where(lane == 0, upright(defocus[...]), 0.0)
    meta = jnp.where(lane == 1, upright(bins[...]), meta)
    meta = jnp.where(lane == 2, 1.0, meta)
    m_own[...] = narrow(jnp.where(lane == 3, CAP * who + rank + 1.0, meta))
    pl.semaphore_wait(barrier, N_MEM - 1 + len(others))

    def rows_of(ref, member):
        return ref.at[pl.ds(pl.multiple_of(member * P_PAD, P_PAD), P_DEV), :]

    def meta_copy(o, owner):
        return pltpu.make_async_remote_copy(
            src_ref=m_own, dst_ref=rows_of(m_buf, owner), send_sem=ms.at[o], recv_sem=mr.at[owner],
            device_id={"mem": peer(o)}, device_id_type=MESH)

    def image_part(q, target):
        return images.at[:, pl.ds(pl.multiple_of(target * WIDTH + q * W, W), W)]

    def image_copy(q, o, owner):
        return pltpu.make_async_remote_copy(
            src_ref=image_part(q, peer(o)), dst_ref=rows_of(x_buf.at[q], owner),
            send_sem=xs.at[q, o], recv_sem=xr.at[q, owner],
            device_id={"mem": peer(o)}, device_id_type=MESH)

    def own_image(q):
        return pltpu.make_async_copy(image_part(q, mem), rows_of(x_buf.at[q], mem), xs.at[q, 0])

    own_meta = pltpu.make_async_copy(m_own, rows_of(m_buf, mem), ms.at[0])
    own_meta.start()

    @pl.loop(1, N_MEM)
    def _(o):
        meta_copy(o, mem).start()

    @pl.loop(0, CHUNKS)
    def _(q):
        own_image(q).start()

        @pl.loop(1, N_MEM)
        def _(o):
            image_copy(q, o, mem).start()

    own_proj = pltpu.make_async_copy(proj.at[:, pl.ds(pl.multiple_of(mem * WIDTH, WIDTH), WIDTH)], pj, pm)
    own_proj.start()

    wide = lax.dot_general(weight[...], spread[...], (((0,), (0,)), ((), ())), preferred_element_type=jnp.float32)
    column = lax.broadcasted_iota(jnp.int32, (RANK, SLOTS), 1).astype(jnp.float32)
    local = column - PART * jnp.floor((column + 0.5) * (1.0 / PART))
    holder = jnp.floor((local + 0.5) * (1.0 / CAP))
    for m in range(N_MEM):
        wt[m * RANK:(m + 1) * RANK, :] = jnp.where(holder == float(m), wide, 0.0).astype(jnp.bfloat16)

    @pl.loop(0, CHUNKS)
    def _(q):
        place = mem * WIDTH + q * W + lax.broadcasted_iota(jnp.int32, (8, W), 1)
        col = place & (SIDE - 1)
        row = lax.shift_right_logical(place, 8)
        fx = jnp.where(col < SIDE // 2, col, col - SIDE).astype(jnp.float32) * (1.0 / SIDE)
        fy = jnp.where(row < SIDE // 2, row, row - SIDE).astype(jnp.float32) * (1.0 / SIDE)
        grid_q[q] = (fx * fx + fy * fy) * (160.0 / (2 * math.pi))

    acc[...] = jnp.zeros_like(acc)

    own_meta.wait()

    @pl.loop(1, N_MEM)
    def _(o):
        owner = peer(N_MEM - o)
        meta_copy(o, peer(o)).wait_recv()

    lane = lax.broadcasted_iota(jnp.int32, (8, 128), 1)
    third = jnp.where(lane == 3, 1.0, 0.0).astype(jnp.bfloat16)
    code = lax.dot_general(third, m_buf[...], (((1,), (1,)), ((), ())), preferred_element_type=jnp.float32)
    which = lax.shift_right_logical(lax.broadcasted_iota(jnp.int32, (1, COLS), 1), 5).astype(jnp.float32)
    code = code[0:1, :] + 64.0 * which
    item = lax.broadcasted_iota(jnp.int32, (PART, COLS), 0).astype(jnp.float32)
    whose = jnp.floor((item + 0.5) * (1.0 / CAP))
    base = whose * 64.0 + (item - CAP * whose) + 1.0 - code
    for c in range(N_CLS):
        sel[c * PART:(c + 1) * PART, :] = jnp.where(base == -float(c * CAP), 1.0, 0.0).astype(jnp.bfloat16)

    def part_of(ref, group):
        return ref.at[pl.ds(pl.multiple_of(group * PART, PART), PART), :]

    def y_copies(src, dst, sems, rsems):
        here = part_of(dst, cls)
        return [pltpu.make_async_remote_copy(
            src_ref=part_of(src, other), dst_ref=here, send_sem=sems.at[i], recv_sem=rsems.at[cls],
            device_id={"cls": other}, device_id_type=MESH) for i, other in enumerate(others)]

    def y_own(src, dst, rsems):
        return pltpu.make_async_copy(part_of(src, cls), part_of(dst, cls), rsems.at[cls])

    def arrivals(dst, sems, rsems):
        for source in others:
            pltpu.make_async_remote_copy(
                src_ref=part_of(dst, source), dst_ref=part_of(dst, source), send_sem=sems.at[0], recv_sem=rsems.at[source],
                device_id={"cls": source}, device_id_type=MESH).wait_recv()

    last = CHUNKS
    smeta[...] = jnp.dot(sel[...], m_buf[...], preferred_element_type=jnp.float32).astype(jnp.bfloat16)
    for copy in y_copies(smeta, rmeta, ys.at[last], yr.at[last]):
        copy.start()
    y_own(smeta, rmeta, yr.at[last]).start()

    def sort(q):
        own_image(q).wait()

        @pl.loop(1, N_MEM)
        def _(o):
            image_copy(q, o, peer(o)).wait_recv()

        send[q] = jnp.dot(sel[...], x_buf[q], preferred_element_type=jnp.float32).astype(jnp.bfloat16)
        for copy in y_copies(send.at[q], recv.at[q], ys.at[q], yr.at[q]):
            copy.start()
        y_own(send.at[q], recv.at[q], yr.at[q]).start()

    def prepare():
        y_own(smeta, rmeta, yr.at[last]).wait()
        arrivals(rmeta, ys.at[last], yr.at[last])
        pick = lax.broadcasted_iota(jnp.int32, (128, 128), 0)
        m = rmeta[...]
        def lanes(i):
            return jnp.dot(m, jnp.where(pick == i, 1.0, 0.0).astype(jnp.bfloat16), preferred_element_type=jnp.float32)
        focus[...] = lanes(0)
        at = lax.broadcasted_iota(jnp.int32, (SLOTS, 128), 1).astype(jnp.float32)
        table[...] = jnp.where((lanes(1) == at) & (lanes(2) == 1.0), 1.0, 0.0).astype(jnp.bfloat16)
        own_proj.wait()

    def consume(q):
        y_own(send.at[q], recv.at[q], yr.at[q]).wait()
        arrivals(recv.at[q], ys.at[q], yr.at[q])
        projected = pj[:, pl.ds(pl.multiple_of(q * W, W), W)]
        chosen[...] = jnp.dot(table[:, 0:8], projected, preferred_element_type=jnp.float32).astype(jnp.bfloat16)

        @pl.loop(0, SLOTS // STRIP, unroll=2)
        def _(i):
            r = pl.ds(pl.multiple_of(i * STRIP, STRIP), STRIP)
            f = focus[r, :]
            for l in range(W // 128):
                cols = slice(l * 128, (l + 1) * 128)
                g = grid_q[q, :, cols]
                turn = f * jnp.concatenate([g] * (STRIP // 8), axis=0) + math.atan(0.1) / (2 * math.pi)
                turn = turn - ((turn + ROUND) - ROUND)
                sq = turn * turn
                value = SINE[5]
                for term in SINE[4::-1]:
                    value = value * sq + term
                ctf = value * turn
                got = recv[q, r, cols].astype(jnp.float32)
                res[q, r, cols] = (got - ctf * chosen[r, cols].astype(jnp.float32)).astype(jnp.bfloat16)

        for n, (i, j) in enumerate(PAIRS):
            acc[n] += dot_t(res[q, i * BLOCK:(i + 1) * BLOCK, :], res[q, j * BLOCK:(j + 1) * BLOCK, :])

    @pl.loop(0, CHUNKS + 2)
    def _(t):
        @pl.when(t < CHUNKS)
        def _():
            sort(t)

        @pl.when(t == 2)
        def _():
            prepare()

        @pl.when(t >= 2)
        def _():
            consume(t - 2)

    for n in range(len(PAIRS)):
        packed[n * BLOCK:(n + 1) * BLOCK, :] = narrow(acc[n])

    def along_x(d):
        return z * 4 + (x + d) % 4

    def along_z(d):
        return ((z + d) % 4) * 4 + x

    axes = [(x, z, along_x, along_z), (z, x, along_z, along_x)]

    def rows(ref, start, size):
        return ref.at[pl.ds(pl.multiple_of(start, 16), size), :]

    def remote(src, dst, s, r, target):
        return pltpu.make_async_remote_copy(src_ref=src, dst_ref=dst, send_sem=s, recv_sem=r,
                                            device_id={"mem": target}, device_id_type=MESH)

    def stage_1(h, d):
        a, b, one, two = axes[h]
        return remote(rows(packed, h * HALF + (a + d) % 4 * FOURTH, FOURTH), first_in.at[h, d - 1],
                      s1.at[h, d - 1], r1.at[h, d - 1], one(d))

    def stage_2(h, d):
        a, b, one, two = axes[h]
        return remote(rows(mid.at[h], (b + d) % 4 * LAST, LAST), second_in.at[h, d - 1],
                      s2.at[h, d - 1], r2.at[h, d - 1], two(d))

    def stage_3(h, d, back=0):
        a, b, one, two = axes[h]
        here = rows(gath, h * HALF + a * FOURTH + (b + back) % 4 * LAST, LAST)
        return remote(here, here, s3.at[h, d - 1], r3.at[h, d - 1], two(d))

    def stage_4(h, d, back=0):
        a, b, one, two = axes[h]
        here = rows(gath, h * HALF + (a + back) % 4 * FOURTH, FOURTH)
        return remote(here, here, s4.at[h, d - 1], r4.at[h, d - 1], one(d))

    def value(ref):
        return ref[...].astype(jnp.float32)

    for d in (2, 1, 3):
        for h in range(2):
            stage_1(h, d).start()
    for h in range(2):
        a, b, one, two = axes[h]
        for d in range(1, 4):
            stage_1(h, d).wait_recv()
        mid[h] = narrow(value(rows(packed, h * HALF + a * FOURTH, FOURTH))
                        + value(first_in.at[h, 0]) + value(first_in.at[h, 1]) + value(first_in.at[h, 2]))
        for d in (2, 1, 3):
            stage_2(h, d).start()
    for h in range(2):
        a, b, one, two = axes[h]
        for d in range(1, 4):
            stage_2(h, d).wait_recv()
        start = pl.multiple_of(h * HALF + a * FOURTH + b * LAST, 16)
        gath[pl.ds(start, LAST), :] = narrow(value(rows(mid.at[h], b * LAST, LAST))
                                             + value(second_in.at[h, 0]) + value(second_in.at[h, 1]) + value(second_in.at[h, 2]))
        for d in (2, 1, 3):
            stage_3(h, d).start()
    for h in range(2):
        for d in range(1, 4):
            stage_3(h, d, -d + 4).wait_recv()
        for d in (2, 1, 3):
            stage_4(h, d).start()
    for h in range(2):
        for d in range(1, 4):
            stage_4(h, d, -d + 4).wait_recv()

    def part(n):
        return gath[n * BLOCK:(n + 1) * BLOCK, :]

    for j in range(SLOTS // BLOCK):
        total = None
        for i in range(SLOTS // BLOCK):
            mine = wt[:, i * BLOCK:(i + 1) * BLOCK]
            one = dot(mine, part(PAIRS.index((i, j)))) if i <= j else dot_t(mine, part(PAIRS.index((j, i))))
            total = one if total is None else total + one
        turned[:, j * BLOCK:(j + 1) * BLOCK] = narrow(total)
    for n, (i, j) in enumerate(QUAD_PAIRS):
        gram[n] = narrow(dot_t(turned[i * BLOCK:(i + 1) * BLOCK, :], wt[j * BLOCK:(j + 1) * BLOCK, :]))

    total = None
    for q, factor in enumerate(merged_factors(lambda i, j: gram[QUAD_PAIRS.index((i, j))])):
        high = narrow(factor)
        here = wt[q * BLOCK:(q + 1) * BLOCK, :]
        one = dot(high, here) + dot(factor - high.astype(jnp.float32), here)
        total = one if total is None else total + one
    coef[...] = narrow(total)

    @pl.loop(0, CHUNKS)
    def _(q):
        out[:, pl.ds(pl.multiple_of(q * W, W), W)] = narrow(dot(coef[...], res[q]))

    @pl.loop(1, N_MEM)
    def _(o):
        meta_copy(o, mem).wait_send()

    for copy in y_copies(smeta, rmeta, ys.at[last], yr.at[last]):
        copy.wait_send()

    @pl.loop(0, CHUNKS)
    def _(q):
        @pl.loop(1, N_MEM)
        def _(o):
            image_copy(q, o, mem).wait_send()

        for copy in y_copies(send.at[q], recv.at[q], ys.at[q], yr.at[q]):
            copy.wait_send()

    for h in range(2):
        for d in range(1, 4):
            for stage in (stage_1, stage_2, stage_3, stage_4):
                stage(h, d).wait_send()


def whole(images, owner, bins, defocus, projections, weight, spread):
    vmem = pl.BlockSpec(memory_space=pltpu.VMEM)
    hbm = pl.BlockSpec(memory_space=pl.ANY)
    bf, f32 = jnp.bfloat16, jnp.float32
    dma = pltpu.SemaphoreType.DMA
    return pl.pallas_call(
        kernel,
        out_shape=jax.ShapeDtypeStruct((RANK, WIDTH), bf),
        in_specs=[hbm, vmem, vmem, vmem, hbm, vmem, vmem],
        out_specs=vmem,
        scratch_shapes=[
            pltpu.VMEM((CHUNKS, COLS, W), bf),
            pltpu.VMEM((P_DEV, 128), bf),
            pltpu.VMEM((COLS, 128), bf),
            pltpu.VMEM((SLOTS, COLS), bf),
            pltpu.VMEM((CHUNKS, SLOTS, W), bf),
            pltpu.VMEM((CHUNKS, SLOTS, W), bf),
            pltpu.VMEM((SLOTS, 128), bf),
            pltpu.VMEM((SLOTS, 128), bf),
            pltpu.VMEM((8, WIDTH), bf),
            pltpu.VMEM((ROWS, SLOTS), bf),
            pltpu.VMEM((SLOTS, 128), f32),
            pltpu.VMEM((SLOTS, 128), bf),
            pltpu.VMEM((CHUNKS, 8, W), f32),
            pltpu.VMEM((SLOTS, W), bf),
            pltpu.VMEM((CHUNKS, SLOTS, W), bf),
            pltpu.VMEM((len(PAIRS), BLOCK, BLOCK), f32),
            pltpu.VMEM((2 * HALF, BLOCK), bf),
            pltpu.VMEM((2, 3, FOURTH, BLOCK), bf),
            pltpu.VMEM((2, FOURTH, BLOCK), bf),
            pltpu.VMEM((2, 3, LAST, BLOCK), bf),
            pltpu.VMEM((2 * HALF, BLOCK), bf),
            pltpu.VMEM((ROWS, SLOTS), bf),
            pltpu.VMEM((len(QUAD_PAIRS), BLOCK, BLOCK), bf),
            pltpu.VMEM((RANK, SLOTS), bf),
            dma((CHUNKS, N_MEM)), dma((CHUNKS, N_MEM)), dma((N_MEM,)), dma((N_MEM,)),
            dma((CHUNKS + 1, N_CLS)), dma((CHUNKS + 1, N_CLS)), dma,
        ] + [dma((2, 3))] * 8,
        compiler_params=pltpu.CompilerParams(collective_id=0, has_side_effects=True, vmem_limit_bytes=60 * 1024 * 1024),
        name="basis",
    )(images, owner, bins, defocus, projections, weight, spread)


def spread_matrix():
    column = np.arange(SLOTS)
    slot = column // PART * CAP + column % CAP
    return (np.arange(N_CLS * CAP)[:, None] == slot[None, :]).astype(np.float32)


def body(images, owner_group, bin_in_group, defocus, projections, sketch_weight):
    spread = jnp.asarray(spread_matrix(), dtype=jnp.bfloat16)
    bins = bin_in_group.reshape(1, P_DEV)
    focus = defocus.reshape(1, P_DEV)
    owner = owner_group.reshape(1, P_DEV)
    return whole(images, owner, bins, focus, projections, sketch_weight.T, spread)[None]


def solution(mesh):
    in_specs = (
        P(("cls", "mem"), None),
        P(("cls", "mem"), None),
        P(("cls", "mem")),
        P(("cls", "mem")),
        P("cls", None),
        P(),
    )
    out_specs = P("cls", None, "mem")
    return jax.shard_map(body, mesh=mesh, in_specs=in_specs, out_specs=out_specs, check_vma=False)
```

profile of v0, /device:TPU:0, one launch (start us, length us, event | category | flops | bytes accessed | tf_op | source)
XLA Modules:
  0.0 131.1 jit_solution(7310754279314413783)
XLA Ops:
  0.0 129.2 %basis.1 = bf16[64,4096]{1,0:T(8,128)(2,1)} custom-call(bf16[24,65536]{1,0:T(8,128)(2,1)} %images.1, s32[1,24]{1,0:T(1,128)} %bitcast.7, s32[1,24]{1,0:T(1,128)} %bitcast.8, bf16[1,24]{1,0:T(2,128)(2,1)} %bitcast.9, bf16[8,65536]{1,0:T(8,128)(2,1)} %proj.1, bf16[48,64]{1,0:T(8,128)(2,1)} %bitcast.6, bf16[48,768]{1,0:T(8,128)(2,1)} %constant.2.clone.spread), custom_call_target="tpu_custom_call" | custom-call | tf_op jit(solution)/shard_map/basis/pallas_call | solution.py:440
  129.3 1.9 %copy.9 = bf16[1,64,4096]{2,1,0:T(8,128)(2,1)} copy(bf16[1,64,4096]{2,1,0:T(8,128)(2,1)} %bitcast.5) | data formatting | bytes 1048576
where the time goes:
time: 131 us
  Pallas kernels  129 us (98%)
  local copies, waits for them, and re-layouts  1.87 us (1%)
    pallas_call x1, Pallas kernels, whole(): pl.pallas_call(kernel, out_shape=jax.ShapeDtypeStruct((RANK, WIDTH), bf),...  129 us

commit v1 on v0

--- a/solution.py
+++ b/solution.py
@@ -27,9 +27,10 @@
 BLOCK = 256
 PAIRS = [(i, j) for i in range(SLOTS // BLOCK) for j in range(i, SLOTS // BLOCK)]
 QUADS = ROWS // BLOCK
-QUAD_PAIRS = [(i, j) for i in range(QUADS) for j in range(i, QUADS)]
-HALF = len(PAIRS) * BLOCK // 2
-FOURTH = HALF // 4
+PIECES = 2
+HALF = len(PAIRS) * BLOCK
+SHARE = HALF // PIECES
+FOURTH = SHARE // 4
 LAST = FOURTH // 4
 MESH = pl.DeviceIdType.MESH
 
@@ -58,61 +59,58 @@
     return lax.dot_general(narrow(a), narrow(b), (((1,), (1,)), ((), ())), preferred_element_type=jnp.float32)
 
 
-def normalise(gram):
-    n = gram.shape[0]
+def normalise(grams):
+    n = grams[0].shape[0]
     row = lax.broadcasted_iota(jnp.int32, (n, n), 0)
     col = lax.broadcasted_iota(jnp.int32, (n, n), 1)
-    diag = jnp.sum(jnp.where(row == col, gram, 0.0), axis=0, keepdims=True)
     same = lax.shift_right_logical(row, 6) == lax.shift_right_logical(col, 6)
-    total = jnp.sum(jnp.where(same, diag, 0.0), axis=1, keepdims=True) + 1e-06
-    g = jnp.where(same, gram, 0.0) / total
-    g2 = dot(g, g)
-    rest = -2.4375 * g + 1.6875 * g2 + dot(g2, -0.5625 * g + 0.0625 * g2)
-    return rest, jnp.sqrt(float(PIX) / total)
-
-
-def advance(gram, factor):
-    rest, scale = normalise(gram)
-    return scale * (2.25 * factor + dot(rest, factor))
-
-
-def merged_factors(block):
-    row = lax.broadcasted_iota(jnp.int32, (BLOCK, BLOCK), 0)
-    col = lax.broadcasted_iota(jnp.int32, (BLOCK, BLOCK), 1)
+    diag = [jnp.sum(jnp.where(row == col, gram, 0.0), axis=0, keepdims=True) for gram in grams]
+    if n == RANK:
+        total = [jnp.sum(d, axis=1, keepdims=True) + 1e-06 for d in diag]
+        g = [gram / t for gram, t in zip(grams, total)]
+    else:
+        total = [jnp.sum(jnp.where(same, d, 0.0), axis=1, keepdims=True) + 1e-06 for d in diag]
+        g = [jnp.where(same, gram, 0.0) / t for gram, t in zip(grams, total)]
+    g2 = [dot(a, a) for a in g]
+    high = [dot(b, -0.5625 * a + 0.0625 * b) for a, b in zip(g, g2)]
+    rest = [-2.4375 * a + 1.6875 * b + c for a, b, c in zip(g, g2, high)]
+    return rest, [jnp.sqrt(float(PIX) / t) for t in total]
+
+
+def advance(turned, factors):
+    grams = [dot_t(t, f) for t, f in zip(turned, factors)]
+    rest, scale = normalise(grams)
+    more = [dot(r, f) for r, f in zip(rest, factors)]
+    return [s * (2.25 * f + m) for s, f, m in zip(scale, factors, more)]
+
+
+def merged(weights, slots, quad_gram):
+    two = 2 * RANK
+    row = lax.broadcasted_iota(jnp.int32, (two, two), 0)
+    col = lax.broadcasted_iota(jnp.int32, (two, two), 1)
     ident = jnp.where(row == col, 1.0, 0.0)
-    chain = []
-    for q in range(QUADS):
-        rest, scale = normalise(block(q, q).astype(jnp.float32))
-        chain.append(scale * (2.25 * ident + rest))
-    for level in range(2):
-        step = RANK << level
-        for q in range(QUADS):
-            d = chain[q]
-            swapped = jnp.concatenate([d[a ^ step:(a ^ step) + step] for a in range(0, BLOCK, step)], axis=0)
-            joined = d + swapped
-            chain[q] = advance(dot_t(dot(joined, block(q, q)), joined), joined)
-    chain = [d[:RANK] for d in chain]
-    size = 2
-    while size <= QUADS:
-        for first in range(0, QUADS, size):
-            group = range(first, first + size)
-            gram = None
-            for j in group:
-                t = None
-                for i in group:
-                    part = dot(chain[i], block(i, j)) if i <= j else dot_t(chain[i], block(j, i))
-                    t = part if t is None else t + part
-                part = dot_t(t, chain[j])
-                gram = part if gram is None else gram + part
-            rest, scale = normalise(gram)
-            for i in group:
-                chain[i] = scale * (2.25 * chain[i] + dot(rest, chain[i]))
-        size *= 2
-    return chain
+    pairs = [quad_gram(q)[a:a + two, a:a + two] for q in range(QUADS) for a in range(0, BLOCK, two)]
+    rest, scale = normalise([p.astype(jnp.float32) for p in pairs])
+    chain = [s * (2.25 * ident + r) for s, r in zip(scale, rest)]
+    chain = [c[:RANK] + c[RANK:] for c in chain]
+    chain = advance([dot(c, p) for c, p in zip(chain, pairs)], chain)
+    chain = [jnp.concatenate([chain[2 * q], chain[2 * q + 1]], axis=1) for q in range(QUADS)]
+    chain = advance([dot(c, quad_gram(q)) for q, c in enumerate(chain)], chain)
+    high = [narrow(c) for c in chain]
+    low = [c - h.astype(jnp.float32) for c, h in zip(chain, high)]
+    spread = [dot(high[q], weights(q)) + dot(low[q], weights(q)) for q in range(QUADS)]
+    factor = jnp.concatenate([spread[q] + spread[q + 1] for q in range(0, QUADS, 2)], axis=0)
+    while True:
+        turned = jnp.concatenate([slots(factor, j) for j in range(SLOTS // BLOCK)], axis=1)
+        factor = advance([turned], [factor])[0]
+        if factor.shape[0] == RANK:
+            return factor
+        half = factor.shape[0] // 2
+        factor = factor[:half] + factor[half:]
 
 
 def kernel(images, owner, bins, defocus, proj, weight, spread, out, x_buf, m_own, m_buf, sel, send, recv, smeta, rmeta,
-           pj, wt, focus, table, grid_q, chosen, res, acc, packed, first_in, mid, second_in, gath, turned, gram, coef,
+           pj, wt, focus, table, grid_q, chosen, res, acc, packed, first_in, mid, second_in, gath, full, turned, gram, coef,
            xs, xr, ms, mr, ys, yr, pm, s1, r1, s2, r2, s3, r3, s4, r4):
     cls = lax.axis_index("cls")
     mem = lax.axis_index("mem")
@@ -316,7 +314,8 @@
             consume(t - 2)
 
     for n in range(len(PAIRS)):
-        packed[n * BLOCK:(n + 1) * BLOCK, :] = narrow(acc[n])
+        for side in range(2):
+            packed[(2 * n + side) * BLOCK:(2 * n + side + 1) * BLOCK, :] = narrow(acc[n, :, side * 128:(side + 1) * 128])
 
     def along_x(d):
         return z * 4 + (x + d) % 4
@@ -325,6 +324,7 @@
         return ((z + d) % 4) * 4 + x
 
     axes = [(x, z, along_x, along_z), (z, x, along_z, along_x)]
+    lines = [(h, k) for k in range(PIECES) for h in range(2)]
 
     def rows(ref, start, size):
         return ref.at[pl.ds(pl.multiple_of(start, 16), size), :]
@@ -333,78 +333,79 @@
         return pltpu.make_async_remote_copy(src_ref=src, dst_ref=dst, send_sem=s, recv_sem=r,
                                             device_id={"mem": target}, device_id_type=MESH)
 
-    def stage_1(h, d):
+    def stage_1(h, k, d):
         a, b, one, two = axes[h]
-        return remote(rows(packed, h * HALF + (a + d) % 4 * FOURTH, FOURTH), first_in.at[h, d - 1],
-                      s1.at[h, d - 1], r1.at[h, d - 1], one(d))
-
-    def stage_2(h, d):
+        return remote(rows(packed, h * HALF + k * SHARE + (a + d) % 4 * FOURTH, FOURTH), first_in.at[h, k, d - 1],
+                      s1.at[h, k, d - 1], r1.at[h, k, d - 1], one(d))
+
+    def stage_2(h, k, d):
         a, b, one, two = axes[h]
-        return remote(rows(mid.at[h], (b + d) % 4 * LAST, LAST), second_in.at[h, d - 1],
-                      s2.at[h, d - 1], r2.at[h, d - 1], two(d))
-
-    def stage_3(h, d, back=0):
+        return remote(rows(mid.at[h, k], (b + d) % 4 * LAST, LAST), second_in.at[h, k, d - 1],
+                      s2.at[h, k, d - 1], r2.at[h, k, d - 1], two(d))
+
+    def stage_3(h, k, d, back=0):
         a, b, one, two = axes[h]
-        here = rows(gath, h * HALF + a * FOURTH + (b + back) % 4 * LAST, LAST)
-        return remote(here, here, s3.at[h, d - 1], r3.at[h, d - 1], two(d))
-
-    def stage_4(h, d, back=0):
+        here = rows(gath, h * HALF + k * SHARE + a * FOURTH + (b + back) % 4 * LAST, LAST)
+        return remote(here, here, s3.at[h, k, d - 1], r3.at[h, k, d - 1], two(d))
+
+    def stage_4(h, k, d, back=0):
         a, b, one, two = axes[h]
-        here = rows(gath, h * HALF + (a + back) % 4 * FOURTH, FOURTH)
-        return remote(here, here, s4.at[h, d - 1], r4.at[h, d - 1], one(d))
+        here = rows(gath, h * HALF + k * SHARE + (a + back) % 4 * FOURTH, FOURTH)
+        return remote(here, here, s4.at[h, k, d - 1], r4.at[h, k, d - 1], one(d))
 
     def value(ref):
         return ref[...].astype(jnp.float32)
 
-    for d in (2, 1, 3):
-        for h in range(2):
-            stage_1(h, d).start()
-    for h in range(2):
+    for h, k in lines:
+        for d in (2, 1, 3):
+            stage_1(h, k, d).start()
+    for h, k in lines:
         a, b, one, two = axes[h]
         for d in range(1, 4):
-            stage_1(h, d).wait_recv()
-        mid[h] = narrow(value(rows(packed, h * HALF + a * FOURTH, FOURTH))
-                        + value(first_in.at[h, 0]) + value(first_in.at[h, 1]) + value(first_in.at[h, 2]))
+            stage_1(h, k, d).wait_recv()
+        mid[h, k] = narrow(value(rows(packed, h * HALF + k * SHARE + a * FOURTH, FOURTH))
+                           + value(first_in.at[h, k, 0]) + value(first_in.at[h, k, 1]) + value(first_in.at[h, k, 2]))
         for d in (2, 1, 3):
-            stage_2(h, d).start()
-    for h in range(2):
+            stage_2(h, k, d).start()
+    for h, k in lines:
         a, b, one, two = axes[h]
         for d in range(1, 4):
-            stage_2(h, d).wait_recv()
-        start = pl.multiple_of(h * HALF + a * FOURTH + b * LAST, 16)
-        gath[pl.ds(start, LAST), :] = narrow(value(rows(mid.at[h], b * LAST, LAST))
-                                             + value(second_in.at[h, 0]) + value(second_in.at[h, 1]) + value(second_in.at[h, 2]))
+            stage_2(h, k, d).wait_recv()
+        start = pl.multiple_of(h * HALF + k * SHARE + a * FOURTH + b * LAST, 16)
+        gath[pl.ds(start, LAST), :] = narrow(value(rows(mid.at[h, k], b * LAST, LAST)) + value(second_in.at[h, k, 0])
+                                             + value(second_in.at[h, k, 1]) + value(second_in.at[h, k, 2]))
         for d in (2, 1, 3):
-            stage_3(h, d).start()
-    for h in range(2):
+            stage_3(h, k, d).start()
+    for h, k in lines:
         for d in range(1, 4):
-            stage_3(h, d, -d + 4).wait_recv()
+            stage_3(h, k, d, -d + 4).wait_recv()
         for d in (2, 1, 3):
-            stage_4(h, d).start()
-    for h in range(2):
+            stage_4(h, k, d).start()
+    for h, k in lines:
         for d in range(1, 4):
-            stage_4(h, d, -d + 4).wait_recv()
-
-    def part(n):
-        return gath[n * BLOCK:(n + 1) * BLOCK, :]
-
-    for j in range(SLOTS // BLOCK):
+            stage_4(h, k, d, -d + 4).wait_recv()
+
+    for n in range(len(PAIRS)):
+        for side in range(2):
+            full[n, :, side * 128:(side + 1) * 128] = gath[(2 * n + side) * BLOCK:(2 * n + side + 1) * BLOCK, :]
+
+    def slots(value, j):
         total = None
         for i in range(SLOTS // BLOCK):
-            mine = wt[:, i * BLOCK:(i + 1) * BLOCK]
-            one = dot(mine, part(PAIRS.index((i, j)))) if i <= j else dot_t(mine, part(PAIRS.index((j, i))))
+            mine = value[:, i * BLOCK:(i + 1) * BLOCK]
+            one = dot(mine, full[PAIRS.index((i, j))]) if i <= j else dot_t(mine, full[PAIRS.index((j, i))])
             total = one if total is None else total + one
-        turned[:, j * BLOCK:(j + 1) * BLOCK] = narrow(total)
-    for n, (i, j) in enumerate(QUAD_PAIRS):
-        gram[n] = narrow(dot_t(turned[i * BLOCK:(i + 1) * BLOCK, :], wt[j * BLOCK:(j + 1) * BLOCK, :]))
-
-    total = None
-    for q, factor in enumerate(merged_factors(lambda i, j: gram[QUAD_PAIRS.index((i, j))])):
-        high = narrow(factor)
-        here = wt[q * BLOCK:(q + 1) * BLOCK, :]
-        one = dot(high, here) + dot(factor - high.astype(jnp.float32), here)
-        total = one if total is None else total + one
-    coef[...] = narrow(total)
+        return total
+
+    for j in range(SLOTS // BLOCK):
+        turned[:, j * BLOCK:(j + 1) * BLOCK] = narrow(slots(wt[...], j))
+
+    def rows_of_quad(ref, q):
+        return ref[q * BLOCK:(q + 1) * BLOCK, :]
+
+    for q in range(QUADS):
+        gram[q] = narrow(dot_t(rows_of_quad(turned, q), rows_of_quad(wt, q)))
+    coef[...] = narrow(merged(lambda q: rows_of_quad(wt, q), slots, lambda q: gram[q]))
 
     @pl.loop(0, CHUNKS)
     def _(q):
@@ -426,10 +427,10 @@
         for copy in y_copies(send.at[q], recv.at[q], ys.at[q], yr.at[q]):
             copy.wait_send()
 
-    for h in range(2):
+    for h, k in lines:
         for d in range(1, 4):
             for stage in (stage_1, stage_2, stage_3, stage_4):
-                stage(h, d).wait_send()
+                stage(h, k, d).wait_send()
 
 
 def whole(images, owner, bins, defocus, projections, weight, spread):
@@ -459,17 +460,18 @@
             pltpu.VMEM((SLOTS, W), bf),
             pltpu.VMEM((CHUNKS, SLOTS, W), bf),
             pltpu.VMEM((len(PAIRS), BLOCK, BLOCK), f32),
-            pltpu.VMEM((2 * HALF, BLOCK), bf),
-            pltpu.VMEM((2, 3, FOURTH, BLOCK), bf),
-            pltpu.VMEM((2, FOURTH, BLOCK), bf),
-            pltpu.VMEM((2, 3, LAST, BLOCK), bf),
-            pltpu.VMEM((2 * HALF, BLOCK), bf),
+            pltpu.VMEM((2 * HALF, 128), bf),
+            pltpu.VMEM((2, PIECES, 3, FOURTH, 128), bf),
+            pltpu.VMEM((2, PIECES, FOURTH, 128), bf),
+            pltpu.VMEM((2, PIECES, 3, LAST, 128), bf),
+            pltpu.VMEM((2 * HALF, 128), bf),
+            pltpu.VMEM((len(PAIRS), BLOCK, BLOCK), bf),
             pltpu.VMEM((ROWS, SLOTS), bf),
-            pltpu.VMEM((len(QUAD_PAIRS), BLOCK, BLOCK), bf),
+            pltpu.VMEM((QUADS, BLOCK, BLOCK), bf),
             pltpu.VMEM((RANK, SLOTS), bf),
             dma((CHUNKS, N_MEM)), dma((CHUNKS, N_MEM)), dma((N_MEM,)), dma((N_MEM,)),
             dma((CHUNKS + 1, N_CLS)), dma((CHUNKS + 1, N_CLS)), dma,
-        ] + [dma((2, 3))] * 8,
+        ] + [dma((2, PIECES, 3))] * 8,
         compiler_params=pltpu.CompilerParams(collective_id=0, has_side_effects=True, vmem_limit_bytes=60 * 1024 * 1024),
         name="basis",
     )(images, owner, bins, defocus, projections, weight, spread)

time: 131 us -> 125 us (0.954)
  Pallas kernels: 129 us -> 123 us
    pallas_call x1, Pallas kernels: 129 us -> 123 us  [whole(): pl.pallas_call(kernel, out_shape=jax.ShapeDtypeStruct((RANK, WIDTH), bf),...]
where the time goes in v1:
time: 125 us
  Pallas kernels  123 us (98%)
  local copies, waits for them, and re-layouts  1.87 us (1%)
    pallas_call x1, Pallas kernels, whole(): pl.pallas_call(kernel, out_shape=jax.ShapeDtypeStruct((RANK, WIDTH), bf),...  123 us

profile of v1, /device:TPU:0, one launch (start us, length us, event | category | flops | bytes accessed | tf_op | source)
XLA Modules:
  0.0 124.8 jit_solution(12794365322322112269)
XLA Ops:
  0.0 122.9 %basis.1 = bf16[64,4096]{1,0:T(8,128)(2,1)} custom-call(bf16[24,65536]{1,0:T(8,128)(2,1)} %images.1, s32[1,24]{1,0:T(1,128)} %bitcast.7, s32[1,24]{1,0:T(1,128)} %bitcast.8, bf16[1,24]{1,0:T(2,128)(2,1)} %bitcast.9, bf16[8,65536]{1,0:T(8,128)(2,1)} %proj.1, bf16[48,64]{1,0:T(8,128)(2,1)} %bitcast.6, bf16[48,768]{1,0:T(8,128)(2,1)} %constant.2.clone.spread), custom_call_target="tpu_custom_call" | custom-call | tf_op jit(solution)/shard_map/basis/pallas_call | solution.py:441
  122.9 1.9 %copy.9 = bf16[1,64,4096]{2,1,0:T(8,128)(2,1)} copy(bf16[1,64,4096]{2,1,0:T(8,128)(2,1)} %bitcast.5) | data formatting | bytes 1048576
